TPU v7x, 32 devices: a whole 2x2x4 slice. The times are simulated.
32 devices in a mesh: gx: 16 (over z, x, core), gy: 2 (over y).
Axes of the slice: x: 2, y: 2, z: 4, core: 2. Of those that a mesh axis runs over, the one named last changes fastest.
Arguments:
- rhs: float32 [16, 2, 4, 320], P('gx', 'gy'), may hold values from -120 to 120
- vol_jac: float32 [16, 2, 4, 320, 320], P('gx', 'gy'), may hold values from -0.3125 to 0.3125
- inv_step: float32 [16, 2, 4], P('gx', 'gy'), may hold values from 4 to 16
- face_jac: float32 [16, 2, 4, 6, 5, 5], P('gx', 'gy'), may hold values from -1 to 1
- orientation: int32 [16, 2, 4, 6], P('gx', 'gy'), may hold values from 0 to 7, as said below
Outputs:
- newton_update: float32 [16, 2, 4, 320], P('gx', 'gy')
- residual_ratio: float32 [], replicated
Inputs may be any that keep to these rules, and one draw needn't show every extreme that they name: `orientation`: the two sides of every face carry inverse codes: where one side has code o, the other has o if o < 4, else 4 + (o & 2) / 2 + 2 (o & 1).
All inputs are finite; a program needn't handle non-finite values.
Results may differ from a plain program's by a relative error of at most 0.0025.
Values sent between devices are 32-bit elements; how exact they have to be, the bound alone decides.
A program may use at most 256 MiB of HBM per device.

v0:
```python
import jax
import jax.numpy as jnp
from jax import lax
from jax.experimental import pallas as pl
from jax.experimental.pallas import tpu as pltpu
from jax.sharding import PartitionSpec as P

Q = 4
NV = 5
ITERS = 3
NS_STEPS = 3
NP = Q**3
FACES = 6
PENALTY = 4.0
SWEEPS = 2**NS_STEPS - 1
MESH = pl.DeviceIdType.MESH
DOWN = 2.0**-40
TINY = 1e-36


def iota(shape, dim):
    return lax.broadcasted_iota(jnp.int32, shape, dim)


def face_coords(node, face):
    first, second, third = node % Q, node // Q % Q, node // (Q * Q)
    pair = [(second, third), (first, third), (first, second)][face // 2]
    return [first, second, third][face // 2], pair[0], pair[1]


def kernel(
    nx, ny, nz,
    vol, rhs_in, face_in, step_in, orient_in,
    out, ratio,
    held_vol, rhs, face, inv_step, orient, mat, aux, wts, own, turn, dinv, basis, dirs, state, halo, packed,
    vol_sem, small_sem, halo_send, halo_recv, sum_send, sum_recv,
):
    gx, gy = lax.axis_index("gx"), lax.axis_index("gy")
    width = nz * NP
    pairs = nz // 2
    sides = 3 if ny == 2 else 4
    lanes = 2 * NP
    me = gx * ny + gy
    small = [
        pltpu.make_async_copy(source, target, small_sem.at[at])
        for at, (source, target) in enumerate(
            [(face_in, face), (orient_in, orient), (step_in, inv_step), (rhs_in, rhs)]
        )
    ]
    for load in small:
        load.start()
    loads = [
        pltpu.make_async_copy(vol.at[0, 0, e], held_vol.at[e], vol_sem.at[e]) for e in range(nz)
    ]
    for load in loads:
        load.start()

    def other(step):
        return (gx + step // ny) % nx, (gy + step % ny) % ny

    barrier = pltpu.get_barrier_semaphore()

    def greet(step, carry):
        pl.semaphore_signal(barrier, inc=1, device_id=other(step), device_id_type=MESH)
        return carry

    lax.fori_loop(1, nx * ny, greet, 0)
    for load in small:
        load.wait()

    basis[...] = jnp.zeros_like(basis)
    for e in range(nz):
        for v in range(NV):
            basis[0, v : v + 1, e * NP : (e + 1) * NP] = (
                rhs[0, 0, e : e + 1, v * NP : (v + 1) * NP] * DOWN
            )
    aux[...] = jnp.zeros_like(aux)
    for e in range(nz):
        for v in range(NV):
            aux[v * 8 : v * 8 + NV, e * FACES : (e + 1) * FACES] = face[:, v, e, :]

    block = iota((FACES * nz, FACES * width), 1) // NP
    wanted_row = block % nz * FACES + block // nz
    spread = (wanted_row == iota((FACES * nz, FACES * width), 0)).astype(jnp.float32)
    line = iota((NV * 8, width), 0)
    same = jnp.where(line // 8 == line % 8, 1.0, 0.0).astype(jnp.float32)
    node = iota((1, width), 1) % NP
    element = iota((1, width), 1) // NP
    step_row = jnp.zeros((1, width), jnp.float32)
    for e in range(nz):
        step_row = jnp.where(element == e, inv_step[0, 0, e], step_row)
    own_part = same * step_row
    expanded = jnp.dot(
        aux[...], spread, precision=lax.Precision.HIGHEST, preferred_element_type=jnp.float32
    )
    for f in range(FACES):
        at = pl.ds(f * width, width)
        weight = 0.5 * expanded[:, f * width : (f + 1) * width] - 0.5 * PENALTY * same
        wts[:, at] = weight
        fixed, first, second = face_coords(node, f)
        covered = fixed == (0 if f % 2 == 0 else Q - 1)
        own_part = own_part + jnp.where(covered, weight + PENALTY * same, 0.0)
        code = jnp.zeros((1, width), jnp.int32)
        for e in range(nz):
            code = jnp.where(element == e, orient[0, 0, e, f], code)
        swap, flip_first, flip_second = (code // 4) % 2, code % 2, (code // 2) % 2
        one = first + swap * (second - first)
        two = second + swap * (first - second)
        one = one + flip_first * (Q - 1 - 2 * one)
        two = two + flip_second * (Q - 1 - 2 * two)
        wanted = jnp.where(covered, one + Q * two + Q * Q * element, -1)
        there = iota((width, 1), 0)
        fixed_m, first_m, second_m = face_coords(there % NP, f ^ 1)
        held = jnp.where(
            fixed_m == (0 if (f ^ 1) % 2 == 0 else Q - 1),
            first_m + Q * second_m + Q * Q * (there // NP),
            -2,
        )
        turn[at, :] = jnp.where(held == wanted, 1.0, 0.0).astype(jnp.bfloat16)
    own[...] = own_part

    for e in range(nz):
        loads[e].wait()
        start = e % 2 * NP
        for v in range(NV):
            mat[e // 2, v, :, start : start + NP] = held_vol[e, :, v * NP : (v + 1) * NP]

    sub = iota((8, lanes), 0)
    low = iota((NP, lanes), 1) < NP
    eye = iota((NP, lanes), 1) % NP == iota((NP, lanes), 0)

    def stack(parts):
        total = jnp.zeros((8, lanes), jnp.float32)
        for v in range(NV):
            total = jnp.where(sub == v, parts[v], total)
        return total

    for p in range(pairs):
        at = slice(p * lanes, (p + 1) * lanes)
        diagonal = stack(
            [
                jnp.sum(
                    jnp.where(eye, mat[p, v, v * NP : (v + 1) * NP, :], 0.0), axis=0, keepdims=True
                )
                for v in range(NV)
            ]
        )
        for v in range(NV):
            diagonal = diagonal + jnp.where(sub == v, own[v * 8 : v * 8 + 8, at], 0.0)
        dinv[:, at] = jnp.where(sub < NV, 1.0 / jnp.where(sub < NV, diagonal, 1.0), 0.0)

    def block_product(value):
        pieces = []
        for p in range(pairs):
            at = slice(p * lanes, (p + 1) * lanes)
            parts = []
            for v in range(NV):
                total = mat[p, 0, v * NP : (v + 1) * NP, :] * value[0:1, at]
                for w in range(1, NV):
                    total = total + mat[p, w, v * NP : (v + 1) * NP, :] * value[w : w + 1, at]
                left = jnp.sum(jnp.where(low, total, 0.0), axis=1, keepdims=True)
                right = jnp.sum(jnp.where(low, 0.0, total), axis=1, keepdims=True)
                placed = jnp.where(eye, jnp.where(low, left, right), 0.0)
                parts.append(jnp.sum(placed, axis=0, keepdims=True))
            total = stack(parts)
            for w in range(NV):
                total = total + own[w * 8 : w * 8 + 8, at] * value[w : w + 1, at]
            pieces.append(total)
        return jnp.concatenate(pieces, axis=1)

    def neighbour_product(states):
        total = jnp.zeros((24, width), jnp.float32)
        for f in range(FACES):
            at = slice(f * width, (f + 1) * width)
            mixed = wts[0:8, at] * states[f][0:1, :]
            for w in range(1, NV):
                mixed = mixed + wts[w * 8 : w * 8 + 8, at] * states[f][w : w + 1, :]
            high = mixed.astype(jnp.bfloat16).astype(jnp.float32)
            rest = mixed - high
            middle = rest.astype(jnp.bfloat16).astype(jnp.float32)
            split = jnp.concatenate([high, middle, rest - middle], axis=0).astype(jnp.bfloat16)
            total = total + jnp.dot(split, turn[at, :], preferred_element_type=jnp.float32)
        return total[0:8] + total[8:16] + total[16:24]

    def sum_copy(step, source, device):
        return pltpu.make_async_remote_copy(
            src_ref=packed.at[me],
            dst_ref=packed.at[source],
            send_sem=sum_send.at[step],
            recv_sem=sum_recv.at[source],
            device_id=device,
            device_id_type=MESH,
        )

    def dot(a, b):
        return jnp.sum(jnp.sum(a * b, axis=0, keepdims=True), axis=1, keepdims=True)

    def halo_copy(step, side):
        targets = [
            ((gx + 1) % nx, gy),
            ((gx + nx - 1) % nx, gy),
            (gx, (gy + 1) % ny),
            (gx, (gy + ny - 1) % ny),
        ]
        return pltpu.make_async_remote_copy(
            src_ref=dirs.at[step],
            dst_ref=halo.at[step, side],
            send_sem=halo_send.at[step, side],
            recv_sem=halo_recv.at[step, side],
            device_id=targets[side],
            device_id_type=MESH,
        )

    def precondition(step):
        state[...] = dinv[...] * basis[step]

        def sweep(_, inner):
            value = state[...]
            state[...] = value + dinv[...] * (basis[step] - block_product(value))
            return inner

        lax.fori_loop(0, SWEEPS, sweep, 0)
        dirs[step] = state[...]

    def apply_jacobian(step, meanwhile=lambda: None):
        for side in range(sides):
            halo_copy(step, side).start()
        direction = dirs[step]
        inner_part = block_product(direction) - basis[step]
        meanwhile()
        for side in range(sides):
            halo_copy(step, side).wait()
        states = [halo[step, min(side, sides - 1)] for side in range(4)]
        states += [pltpu.roll(direction, NP, 1), pltpu.roll(direction, width - NP, 1)]
        basis[step + 1] = inner_part + neighbour_product(states)

    precondition(0)
    pl.semaphore_wait(barrier, nx * ny - 1)

    def iteration(step, carry):
        apply_jacobian(step)
        precondition(step + 1)
        return carry

    lax.fori_loop(0, ITERS - 1, iteration, 0)

    count = ITERS + 1
    where = iota((1, lanes), 1)
    zeros = jnp.zeros((1, lanes), jnp.float32)
    slots = {}
    for j in range(count):
        for i in range(j + 1):
            slots[i, j] = len(slots)
    peaks = []
    scaled = []
    rows = [zeros, zeros, zeros]

    def add_products(j):
        vector = basis[j]
        peak = jnp.max(jnp.max(jnp.abs(vector), axis=0, keepdims=True), axis=1, keepdims=True)
        peaks.append(peak)
        scaled.append(vector * jnp.where(peak > TINY, 1.0 / jnp.maximum(peak, TINY), 0.0))
        for i in range(j + 1):
            chosen = where == slots[i, j]
            for at, entry in enumerate([dot(scaled[i], scaled[j]), peaks[i], peaks[j]]):
                rows[at] = jnp.where(chosen, entry, rows[at])

    apply_jacobian(ITERS - 1, lambda: [add_products(j) for j in range(ITERS)])
    add_products(ITERS)
    row, row_peak, column_peak = rows
    packed[me, :, 0:lanes] = row
    packed[me, :, lanes : 2 * lanes] = row_peak
    packed[me, :, 2 * lanes : 3 * lanes] = column_peak

    def send(step, carry):
        sum_copy(step, me, other(step)).start()
        return carry

    def take(step, carry):
        there = other(step)
        sum_copy(step, there[0] * ny + there[1], there).wait()
        return carry

    lax.fori_loop(1, nx * ny, send, 0)
    lax.fori_loop(1, nx * ny, take, 0)
    row_peaks = packed[:, :, lanes : 2 * lanes]
    column_peaks = packed[:, :, 2 * lanes : 3 * lanes]
    row_peak = jnp.max(row_peaks, axis=0)
    column_peak = jnp.max(column_peaks, axis=0)
    shares = (row_peaks * (1.0 / jnp.maximum(row_peak, TINY))) * (
        column_peaks * (1.0 / jnp.maximum(column_peak, TINY))
    )
    row = jnp.sum(packed[:, :, 0:lanes] * shares, axis=0)
    gram = {key: row[:, at : at + 1] for key, at in slots.items()}
    sizes = [row_peak[:, slots[i, i] : slots[i, i] + 1] for i in range(count)]
    upper = {}
    for i in range(count):
        for j in range(i, count):
            left = gram[i, j]
            for k in range(i):
                left = left - upper[k, i] * upper[k, j]
            upper[i, j] = jnp.sqrt(jnp.maximum(left, 0.0)) if i == j else left / upper[i, i]
    grown = [sizes[j + 1] / sizes[j] for j in range(ITERS)]
    zero = jnp.zeros((1, 1), jnp.float32)

    target = [upper[0, 0]] + [zero] * ITERS
    rotations = []
    columns = []
    for j in range(ITERS):
        column = [
            upper.get((i, j), zero) + grown[j] * upper[i, j + 1] for i in range(j + 2)
        ]
        for i in range(j):
            cosine, sine = rotations[i]
            column[i], column[i + 1] = (
                cosine * column[i] + sine * column[i + 1],
                cosine * column[i + 1] - sine * column[i],
            )
        radius = jnp.sqrt(column[j] * column[j] + column[j + 1] * column[j + 1])
        cosine, sine = column[j] / radius, column[j + 1] / radius
        rotations.append((cosine, sine))
        column[j] = radius
        target[j + 1] = -sine * target[j]
        target[j] = cosine * target[j]
        columns.append(column)
    solved = [None] * ITERS
    for i in reversed(range(ITERS)):
        left = target[i]
        for j in range(i + 1, ITERS):
            left = left - columns[j][i] * solved[j]
        solved[i] = left / columns[i][i]
    ratio[...] = jnp.abs(target[ITERS]) / upper[0, 0]
    update = solved[0] * (dirs[0] * (1.0 / DOWN))
    for j in range(1, ITERS):
        update = update + solved[j] * (dirs[j] * (sizes[0] / DOWN / sizes[j]))
    for e in range(nz):
        for v in range(NV):
            out[0, 0, e : e + 1, v * NP : (v + 1) * NP] = update[
                v : v + 1, e * NP : (e + 1) * NP
            ]


def solution(mesh):
    nx, ny = mesh.shape["gx"], mesh.shape["gy"]

    def body(rhs, vol_jac, inv_step, face_jac, orientation):
        nz = rhs.shape[2]
        width = nz * NP
        face = jnp.transpose(face_jac[0, 0], (2, 3, 0, 1))
        f32 = jnp.float32
        vmem = pl.BlockSpec(memory_space=pltpu.VMEM)
        dma = pltpu.SemaphoreType.DMA
        update, ratio = pl.pallas_call(
            lambda *refs: kernel(nx, ny, nz, *refs),
            out_shape=(
                jax.ShapeDtypeStruct(rhs.shape, f32),
                jax.ShapeDtypeStruct((1, 1), f32),
            ),
            in_specs=[pl.BlockSpec(memory_space=pl.ANY)] * 5,
            out_specs=(vmem, vmem),
            scratch_shapes=[
                pltpu.VMEM((nz, NV * NP, NV * NP), f32),
                pltpu.VMEM(rhs.shape, f32),
                pltpu.VMEM(face.shape, f32),
                pltpu.SMEM(inv_step.shape, f32),
                pltpu.SMEM(orientation.shape, jnp.int32),
                pltpu.VMEM((nz // 2, NV, NV * NP, 2 * NP), f32),
                pltpu.VMEM((NV * 8, FACES * nz), f32),
                pltpu.VMEM((NV * 8, FACES * width), f32),
                pltpu.VMEM((NV * 8, width), f32),
                pltpu.VMEM((FACES * width, width), jnp.bfloat16),
                pltpu.VMEM((8, width), f32),
                pltpu.VMEM((ITERS + 1, 8, width), f32),
                pltpu.VMEM((ITERS, 8, width), f32),
                pltpu.VMEM((8, width), f32),
                pltpu.VMEM((ITERS, 4, 8, width), f32),
                pltpu.VMEM((nx * ny, 1, 6 * NP), f32),
                dma((nz,)),
                dma((4,)),
                dma((ITERS, 4)),
                dma((ITERS, 4)),
                dma((nx * ny,)),
                dma((nx * ny,)),
            ],
            compiler_params=pltpu.CompilerParams(collective_id=0, has_side_effects=True),
            name="newton_step",
        )(vol_jac, rhs, face, inv_step, orientation)
        return update, ratio[0, 0]

    placed = (
        P("gx", "gy", None, None),
        P("gx", "gy", None, None, None),
        P("gx", "gy", None),
        P("gx", "gy", None, None, None, None),
        P("gx", "gy", None, None),
    )
    return jax.shard_map(
        body,
        mesh=mesh,
        in_specs=placed,
        out_specs=(P("gx", "gy", None, None), P()),
        check_vma=False,
    )
```

profile of v0, /device:TPU:0, one launch (start us, length us, event | category | flops | bytes accessed | tf_op | source)
XLA Modules:
  0.0 32.6 jit_solution(16846489626773763019)
XLA Ops:
  0.6 28.9 %newton_step.1 = (f32[1,1,4,320]{3,2,1,0:T(4,128)}, f32[1,1]{1,0:T(1,128)}) custom-call(f32[1,1,4,320,320]{4,3,2,1,0:T(8,128)} %refs_0_.1, f32[1,1,4,320]{3,2,1,0:T(4,128)} %refs_1_.1, f32[5,5,4,6]{3,2,1,0:T(4,128)} %bitcast.4, f32[1,1,4]{2,1,0:T(1,128)} %refs_3_.1, s32[1,1,4,6]{3,2,1,0:T(4,128)} %refs_4_.1), custom_call_target="tpu_custom_call" | custom-call | tf_op jit(solution)/shard_map/newton_step/pallas_call | solution.py:353
  29.6 1.3 %copy.9 = f32[1,1,4,320]{3,2,1,0:T(4,128)} copy(f32[1,1,4,320]{3,2,1,0:T(4,128)} %get-tuple-element.8) | data formatting | bytes 10240
where the time goes:
time: 32.8 us; the launch traced here: 32.6 us
  Pallas kernels  28.9 us (88%)
  between operations  2.4 us (7%)
  local copies, waits for them, and re-layouts  1.29 us (4%)
    pallas_call x1, Pallas kernels, body(): pl.pallas_call(lambda *refs: kernel(nx, ny, nz, *refs), out_shape=(jax.Sh...  28.9 us
    unnamed x1, local copies, waits for them, and re-layouts  1.29 us

commit v1 on v0

--- a/solution.py
+++ b/solution.py
@@ -10,22 +10,30 @@
 ITERS = 3
 NS_STEPS = 3
 NP = Q**3
+BLK = NV * NP
 FACES = 6
+AXES = 3
 PENALTY = 4.0
 SWEEPS = 2**NS_STEPS - 1
 MESH = pl.DeviceIdType.MESH
 DOWN = 2.0**-40
 TINY = 1e-36
+UNROLL = 64
 
 
 def iota(shape, dim):
     return lax.broadcasted_iota(jnp.int32, shape, dim)
 
 
-def face_coords(node, face):
+def axis_coords(node, axis):
     first, second, third = node % Q, node // Q % Q, node // (Q * Q)
-    pair = [(second, third), (first, third), (first, second)][face // 2]
-    return [first, second, third][face // 2], pair[0], pair[1]
+    pair = [(second, third), (first, third), (first, second)][axis]
+    return [first, second, third][axis], pair[0], pair[1]
+
+
+def node_of(axis, fixed, one, two):
+    first, second, third = [(fixed, one, two), (one, fixed, two), (one, two, fixed)][axis]
+    return first + Q * second + Q * Q * third
 
 
 def kernel(
@@ -33,14 +41,19 @@
     vol, rhs_in, face_in, step_in, orient_in,
     out, ratio,
     held_vol, rhs, face, inv_step, orient, mat, aux, wts, own, turn, dinv, basis, dirs, state, halo, packed,
+    series, fourth, left_op, right_op,
     vol_sem, small_sem, halo_send, halo_recv, sum_send, sum_recv,
 ):
     gx, gy = lax.axis_index("gx"), lax.axis_index("gy")
+    devices = nx * ny
     width = nz * NP
     pairs = nz // 2
     sides = 3 if ny == 2 else 4
     lanes = 2 * NP
     me = gx * ny + gy
+    loads = [
+        pltpu.make_async_copy(vol.at[0, 0, e], held_vol.at[e], vol_sem.at[e]) for e in range(nz)
+    ]
     small = [
         pltpu.make_async_copy(source, target, small_sem.at[at])
         for at, (source, target) in enumerate(
@@ -49,43 +62,57 @@
     ]
     for load in small:
         load.start()
-    loads = [
-        pltpu.make_async_copy(vol.at[0, 0, e], held_vol.at[e], vol_sem.at[e]) for e in range(nz)
-    ]
     for load in loads:
         load.start()
 
-    def other(step):
-        return (gx + step // ny) % nx, (gy + step % ny) % ny
+    def other(along, across):
+        return lax.rem(gx + along, nx), lax.rem(gy + across, ny)
+
+    def each_other(visit):
+        if devices <= UNROLL:
+            for step in range(1, devices):
+                visit(step // ny, step % ny)
+        else:
+            def several(step, carry):
+                visit(step // ny, step % ny)
+                return carry
+
+            lax.fori_loop(1, devices, several, 0)
 
     barrier = pltpu.get_barrier_semaphore()
 
-    def greet(step, carry):
-        pl.semaphore_signal(barrier, inc=1, device_id=other(step), device_id_type=MESH)
-        return carry
-
-    lax.fori_loop(1, nx * ny, greet, 0)
+    def greet(along, across):
+        pl.semaphore_signal(barrier, inc=1, device_id=other(along, across), device_id_type=MESH)
+
+    each_other(greet)
+
+    node = iota((1, width), 1) % NP
+    element = iota((1, width), 1) // NP
+    row = iota((FACES * nz, width), 0)
+    spreads = []
+    covers = []
+    for axis in range(AXES):
+        fixed = axis_coords(node, axis)[0]
+        covered = (fixed == 0) | (fixed == Q - 1)
+        covers.append(covered)
+        wanted = element * FACES + 2 * axis + jnp.where(fixed == 0, 0, 1)
+        spreads.append(jnp.where(covered & (row == wanted), 1.0, 0.0).astype(jnp.float32))
+    spread = jnp.concatenate(spreads, axis=1)
+    aux[...] = jnp.zeros_like(aux)
+    basis[...] = jnp.zeros_like(basis)
+
     for load in small:
         load.wait()
-
-    basis[...] = jnp.zeros_like(basis)
     for e in range(nz):
         for v in range(NV):
             basis[0, v : v + 1, e * NP : (e + 1) * NP] = (
                 rhs[0, 0, e : e + 1, v * NP : (v + 1) * NP] * DOWN
             )
-    aux[...] = jnp.zeros_like(aux)
     for e in range(nz):
         for v in range(NV):
             aux[v * 8 : v * 8 + NV, e * FACES : (e + 1) * FACES] = face[:, v, e, :]
-
-    block = iota((FACES * nz, FACES * width), 1) // NP
-    wanted_row = block % nz * FACES + block // nz
-    spread = (wanted_row == iota((FACES * nz, FACES * width), 0)).astype(jnp.float32)
     line = iota((NV * 8, width), 0)
     same = jnp.where(line // 8 == line % 8, 1.0, 0.0).astype(jnp.float32)
-    node = iota((1, width), 1) % NP
-    element = iota((1, width), 1) // NP
     step_row = jnp.zeros((1, width), jnp.float32)
     for e in range(nz):
         step_row = jnp.where(element == e, inv_step[0, 0, e], step_row)
@@ -93,30 +120,25 @@
     expanded = jnp.dot(
         aux[...], spread, precision=lax.Precision.HIGHEST, preferred_element_type=jnp.float32
     )
-    for f in range(FACES):
-        at = pl.ds(f * width, width)
-        weight = 0.5 * expanded[:, f * width : (f + 1) * width] - 0.5 * PENALTY * same
-        wts[:, at] = weight
-        fixed, first, second = face_coords(node, f)
-        covered = fixed == (0 if f % 2 == 0 else Q - 1)
-        own_part = own_part + jnp.where(covered, weight + PENALTY * same, 0.0)
+    for axis in range(AXES):
+        at = slice(axis * width, (axis + 1) * width)
+        half = 0.5 * expanded[:, at]
+        jump = jnp.where(covers[axis], 0.5 * PENALTY * same, 0.0)
+        wts[:, at] = half - jump
+        own_part = own_part + (half + jump)
+        fixed, first, second = axis_coords(node, axis)
         code = jnp.zeros((1, width), jnp.int32)
         for e in range(nz):
-            code = jnp.where(element == e, orient[0, 0, e, f], code)
+            side = jnp.where(fixed == 0, orient[0, 0, e, 2 * axis], orient[0, 0, e, 2 * axis + 1])
+            code = jnp.where(element == e, side, code)
         swap, flip_first, flip_second = (code // 4) % 2, code % 2, (code // 2) % 2
         one = first + swap * (second - first)
         two = second + swap * (first - second)
         one = one + flip_first * (Q - 1 - 2 * one)
         two = two + flip_second * (Q - 1 - 2 * two)
-        wanted = jnp.where(covered, one + Q * two + Q * Q * element, -1)
-        there = iota((width, 1), 0)
-        fixed_m, first_m, second_m = face_coords(there % NP, f ^ 1)
-        held = jnp.where(
-            fixed_m == (0 if (f ^ 1) % 2 == 0 else Q - 1),
-            first_m + Q * second_m + Q * Q * (there // NP),
-            -2,
-        )
-        turn[at, :] = jnp.where(held == wanted, 1.0, 0.0).astype(jnp.bfloat16)
+        there = jnp.where(covers[axis], node_of(axis, Q - 1 - fixed, one, two), node)
+        there = there + (element % 2) * NP
+        turn[:, at] = jnp.broadcast_to(there, (8, width))
     own[...] = own_part
 
     for e in range(nz):
@@ -149,45 +171,103 @@
             diagonal = diagonal + jnp.where(sub == v, own[v * 8 : v * 8 + 8, at], 0.0)
         dinv[:, at] = jnp.where(sub < NV, 1.0 / jnp.where(sub < NV, diagonal, 1.0), 0.0)
 
+    def dense_product(blocks, value, p):
+        at = slice(p * lanes, (p + 1) * lanes)
+        parts = []
+        for v in range(NV):
+            total = blocks[p, 0, v * NP : (v + 1) * NP, :] * value[0:1, at]
+            for w in range(1, NV):
+                total = total + blocks[p, w, v * NP : (v + 1) * NP, :] * value[w : w + 1, at]
+            left = jnp.sum(jnp.where(low, total, 0.0), axis=1, keepdims=True)
+            right = jnp.sum(jnp.where(low, 0.0, total), axis=1, keepdims=True)
+            placed = jnp.where(eye, jnp.where(low, left, right), 0.0)
+            parts.append(jnp.sum(placed, axis=0, keepdims=True))
+        return stack(parts)
+
+    def series_product(blocks, value):
+        return jnp.concatenate([dense_product(blocks, value, p) for p in range(pairs)], axis=1)
+
     def block_product(value):
         pieces = []
         for p in range(pairs):
             at = slice(p * lanes, (p + 1) * lanes)
-            parts = []
-            for v in range(NV):
-                total = mat[p, 0, v * NP : (v + 1) * NP, :] * value[0:1, at]
-                for w in range(1, NV):
-                    total = total + mat[p, w, v * NP : (v + 1) * NP, :] * value[w : w + 1, at]
-                left = jnp.sum(jnp.where(low, total, 0.0), axis=1, keepdims=True)
-                right = jnp.sum(jnp.where(low, 0.0, total), axis=1, keepdims=True)
-                placed = jnp.where(eye, jnp.where(low, left, right), 0.0)
-                parts.append(jnp.sum(placed, axis=0, keepdims=True))
-            total = stack(parts)
+            total = dense_product(mat, value, p)
             for w in range(NV):
                 total = total + own[w * 8 : w * 8 + 8, at] * value[w : w + 1, at]
             pieces.append(total)
         return jnp.concatenate(pieces, axis=1)
 
-    def neighbour_product(states):
-        total = jnp.zeros((24, width), jnp.float32)
-        for f in range(FACES):
-            at = slice(f * width, (f + 1) * width)
-            mixed = wts[0:8, at] * states[f][0:1, :]
+    def face_product(axis, before, after):
+        fixed = axis_coords(iota((8, width), 1) % NP, axis)[0]
+        joined = jnp.where(fixed == Q - 1, before, after)
+        pieces = []
+        for p in range(pairs):
+            at = slice(p * lanes, (p + 1) * lanes)
+            here = slice(axis * width + p * lanes, axis * width + (p + 1) * lanes)
+            turned = jnp.take_along_axis(
+                joined[:, at], turn[:, here], axis=1, mode="promise_in_bounds"
+            )
+            total = wts[0:8, here] * turned[0:1, :]
             for w in range(1, NV):
-                mixed = mixed + wts[w * 8 : w * 8 + 8, at] * states[f][w : w + 1, :]
-            high = mixed.astype(jnp.bfloat16).astype(jnp.float32)
-            rest = mixed - high
-            middle = rest.astype(jnp.bfloat16).astype(jnp.float32)
-            split = jnp.concatenate([high, middle, rest - middle], axis=0).astype(jnp.bfloat16)
-            total = total + jnp.dot(split, turn[at, :], preferred_element_type=jnp.float32)
-        return total[0:8] + total[8:16] + total[16:24]
-
-    def sum_copy(step, source, device):
+                total = total + wts[w * 8 : w * 8 + 8, here] * turned[w : w + 1, :]
+            pieces.append(total)
+        return jnp.concatenate(pieces, axis=1)
+
+    def put_right(p, v, w, tile):
+        cut = slice(w * lanes, (w + 1) * lanes)
+        upper, lower = slice(v * lanes, v * lanes + NP), slice(v * lanes + NP, (v + 1) * lanes)
+        right_op[p, upper, cut] = jnp.where(low, tile, 0.0).astype(jnp.bfloat16)
+        right_op[p, lower, cut] = jnp.where(low, 0.0, tile).astype(jnp.bfloat16)
+
+    def first_powers():
+        for p in range(pairs):
+            for w in range(NV):
+                at = slice(p * lanes, (p + 1) * lanes)
+                for v in range(NV):
+                    rows = slice(v * NP, (v + 1) * NP)
+                    tile = mat[p, w, rows, :]
+                    if v == w:
+                        tile = jnp.where(eye, 0.0, tile)
+                    else:
+                        tile = tile + jnp.where(eye, own[w * 8 + v : w * 8 + v + 1, at], 0.0)
+                    tile = -tile * dinv[w : w + 1, at]
+                    series[p, w, rows, :] = tile
+                    left_op[p, rows, w * lanes : (w + 1) * lanes] = tile.astype(jnp.bfloat16)
+                    put_right(p, v, w, tile)
+        for p in range(pairs):
+            square = jnp.dot(left_op[p, 0:BLK, :], right_op[p], preferred_element_type=jnp.float32)
+            for w in range(NV):
+                cut = slice(w * lanes, (w + 1) * lanes)
+                series[p, w] = series[p, w] + square[:, cut]
+                left_op[p, BLK : 2 * BLK, cut] = square[:, cut].astype(jnp.bfloat16)
+                for v in range(NV):
+                    put_right(p, v, w, square[v * NP : (v + 1) * NP, cut])
+        for p in range(pairs):
+            both = jnp.dot(left_op[p], right_op[p], preferred_element_type=jnp.float32)
+            for w in range(NV):
+                cut = slice(w * lanes, (w + 1) * lanes)
+                series[p, w] = series[p, w] + both[0:BLK, cut]
+                fourth[p, w] = both[BLK : 2 * BLK, cut]
+
+    def all_powers():
+        for p in range(pairs):
+            for w in range(NV):
+                cut = slice(w * lanes, (w + 1) * lanes)
+                left_op[p, 0:BLK, cut] = fourth[p, w].astype(jnp.bfloat16)
+                for v in range(NV):
+                    put_right(p, v, w, series[p, w, v * NP : (v + 1) * NP, :])
+        for p in range(pairs):
+            last = jnp.dot(left_op[p, 0:BLK, :], right_op[p], preferred_element_type=jnp.float32)
+            for w in range(NV):
+                cut = slice(w * lanes, (w + 1) * lanes)
+                series[p, w] = series[p, w] + (fourth[p, w] + last[:, cut])
+
+    def sum_copy(device):
         return pltpu.make_async_remote_copy(
             src_ref=packed.at[me],
-            dst_ref=packed.at[source],
-            send_sem=sum_send.at[step],
-            recv_sem=sum_recv.at[source],
+            dst_ref=packed.at[me],
+            send_sem=sum_send,
+            recv_sem=sum_recv,
             device_id=device,
             device_id_type=MESH,
         )
@@ -197,10 +277,10 @@
 
     def halo_copy(step, side):
         targets = [
-            ((gx + 1) % nx, gy),
-            ((gx + nx - 1) % nx, gy),
-            (gx, (gy + 1) % ny),
-            (gx, (gy + ny - 1) % ny),
+            (lax.rem(gx + 1, nx), gy),
+            (lax.rem(gx + nx - 1, nx), gy),
+            (gx, lax.rem(gy + 1, ny)),
+            (gx, lax.rem(gy + ny - 1, ny)),
         ]
         return pltpu.make_async_remote_copy(
             src_ref=dirs.at[step],
@@ -211,38 +291,41 @@
             device_id_type=MESH,
         )
 
-    def precondition(step):
-        state[...] = dinv[...] * basis[step]
-
-        def sweep(_, inner):
-            value = state[...]
-            state[...] = value + dinv[...] * (basis[step] - block_product(value))
-            return inner
-
-        lax.fori_loop(0, SWEEPS, sweep, 0)
-        dirs[step] = state[...]
-
-    def apply_jacobian(step, meanwhile=lambda: None):
+    def apply_jacobian(step, meanwhile):
         for side in range(sides):
             halo_copy(step, side).start()
         direction = dirs[step]
         inner_part = block_product(direction) - basis[step]
+        before, after = pltpu.roll(direction, NP, 1), pltpu.roll(direction, width - NP, 1)
+        inner_part = inner_part + face_product(2, before, after)
         meanwhile()
         for side in range(sides):
             halo_copy(step, side).wait()
-        states = [halo[step, min(side, sides - 1)] for side in range(4)]
-        states += [pltpu.roll(direction, NP, 1), pltpu.roll(direction, width - NP, 1)]
-        basis[step + 1] = inner_part + neighbour_product(states)
-
-    precondition(0)
-    pl.semaphore_wait(barrier, nx * ny - 1)
-
-    def iteration(step, carry):
-        apply_jacobian(step)
-        precondition(step + 1)
-        return carry
-
-    lax.fori_loop(0, ITERS - 1, iteration, 0)
+        basis[step + 1] = (
+            inner_part
+            + face_product(0, halo[step, 0], halo[step, 1])
+            + face_product(1, halo[step, 2], halo[step, sides - 1])
+        )
+
+    state[...] = dinv[...] * basis[0]
+
+    def sweep(_, inner):
+        value = state[...]
+        state[...] = value + dinv[...] * (basis[0] - block_product(value))
+        return inner
+
+    lax.fori_loop(0, SWEEPS, sweep, 0)
+    dirs[0] = state[...]
+    pl.semaphore_wait(barrier, devices - 1)
+    apply_jacobian(0, first_powers)
+
+    vector = basis[1]
+    vector = vector + series_product(series, vector)
+    dirs[1] = dinv[...] * (vector + series_product(fourth, vector))
+    apply_jacobian(1, all_powers)
+
+    vector = basis[2]
+    dirs[2] = dinv[...] * (vector + series_product(series, vector))
 
     count = ITERS + 1
     where = iota((1, lanes), 1)
@@ -272,17 +355,10 @@
     packed[me, :, lanes : 2 * lanes] = row_peak
     packed[me, :, 2 * lanes : 3 * lanes] = column_peak
 
-    def send(step, carry):
-        sum_copy(step, me, other(step)).start()
-        return carry
-
-    def take(step, carry):
-        there = other(step)
-        sum_copy(step, there[0] * ny + there[1], there).wait()
-        return carry
-
-    lax.fori_loop(1, nx * ny, send, 0)
-    lax.fori_loop(1, nx * ny, take, 0)
+    each_other(lambda along, across: sum_copy(other(along, across)).start())
+    arrived = packed.at[pl.ds(0, devices - 1)]
+    pltpu.make_async_copy(arrived, arrived, sum_recv).wait()
+    pltpu.make_async_copy(arrived, arrived, sum_send).wait()
     row_peaks = packed[:, :, lanes : 2 * lanes]
     column_peaks = packed[:, :, 2 * lanes : 3 * lanes]
     row_peak = jnp.max(row_peaks, axis=0)
@@ -366,21 +442,25 @@
                 pltpu.SMEM(orientation.shape, jnp.int32),
                 pltpu.VMEM((nz // 2, NV, NV * NP, 2 * NP), f32),
                 pltpu.VMEM((NV * 8, FACES * nz), f32),
-                pltpu.VMEM((NV * 8, FACES * width), f32),
+                pltpu.VMEM((NV * 8, AXES * width), f32),
                 pltpu.VMEM((NV * 8, width), f32),
-                pltpu.VMEM((FACES * width, width), jnp.bfloat16),
+                pltpu.VMEM((8, AXES * width), jnp.int32),
                 pltpu.VMEM((8, width), f32),
                 pltpu.VMEM((ITERS + 1, 8, width), f32),
                 pltpu.VMEM((ITERS, 8, width), f32),
                 pltpu.VMEM((8, width), f32),
                 pltpu.VMEM((ITERS, 4, 8, width), f32),
                 pltpu.VMEM((nx * ny, 1, 6 * NP), f32),
+                pltpu.VMEM((nz // 2, NV, NV * NP, 2 * NP), f32),
+                pltpu.VMEM((nz // 2, NV, NV * NP, 2 * NP), f32),
+                pltpu.VMEM((nz // 2, 2 * BLK, 2 * BLK), jnp.bfloat16),
+                pltpu.VMEM((nz // 2, 2 * BLK, 2 * BLK), jnp.bfloat16),
                 dma((nz,)),
                 dma((4,)),
                 dma((ITERS, 4)),
                 dma((ITERS, 4)),
-                dma((nx * ny,)),
-                dma((nx * ny,)),
+                dma,
+                dma,
             ],
             compiler_params=pltpu.CompilerParams(collective_id=0, has_side_effects=True),
             name="newton_step",

time: 32.8 us -> 28.8 us (0.88)
  Pallas kernels: 28.9 us -> 24.9 us
    pallas_call x1, Pallas kernels: 28.9 us -> 24.9 us  [body(): pl.pallas_call(lambda *refs: kernel(nx, ny, nz, *refs), out_shape=(jax.Sh...]
where the time goes in v1:
time: 28.8 us; the launch traced here: 28.6 us
  Pallas kernels  24.9 us (86%)
  between operations  2.4 us (8%)
  local copies, waits for them, and re-layouts  1.29 us (4%)
    pallas_call x1, Pallas kernels, body(): pl.pallas_call(lambda *refs: kernel(nx, ny, nz, *refs), out_shape=(jax.Sh...  24.9 us
    unnamed x1, local copies, waits for them, and re-layouts  1.29 us

profile of v1, /device:TPU:0, one launch (start us, length us, event | category | flops | bytes accessed | tf_op | source)
XLA Modules:
  0.0 28.6 jit_solution(4568704894894031951)
XLA Ops:
  0.6 24.9 %newton_step.1 = (f32[1,1,4,320]{3,2,1,0:T(4,128)}, f32[1,1]{1,0:T(1,128)}) custom-call(f32[1,1,4,320,320]{4,3,2,1,0:T(8,128)} %refs_0_.1, f32[1,1,4,320]{3,2,1,0:T(4,128)} %refs_1_.1, f32[5,5,4,6]{3,2,1,0:T(4,128)} %bitcast.4, f32[1,1,4]{2,1,0:T(1,128)} %refs_3_.1, s32[1,1,4,6]{3,2,1,0:T(4,128)} %refs_4_.1), custom_call_target="tpu_custom_call" | custom-call | tf_op jit(solution)/shard_map/newton_step/pallas_call | solution.py:429
  25.6 1.3 %copy.9 = f32[1,1,4,320]{3,2,1,0:T(4,128)} copy(f32[1,1,4,320]{3,2,1,0:T(4,128)} %get-tuple-element.8) | data formatting | bytes 10240

commit v2 on v1

--- a/solution.py
+++ b/solution.py
@@ -14,7 +14,6 @@
 FACES = 6
 AXES = 3
 PENALTY = 4.0
-SWEEPS = 2**NS_STEPS - 1
 MESH = pl.DeviceIdType.MESH
 DOWN = 2.0**-40
 TINY = 1e-36
@@ -40,8 +39,8 @@
     nx, ny, nz,
     vol, rhs_in, face_in, step_in, orient_in,
     out, ratio,
-    held_vol, rhs, face, inv_step, orient, mat, aux, wts, own, turn, dinv, basis, dirs, state, halo, packed,
-    series, fourth, left_op, right_op,
+    held_vol, rhs, face, inv_step, orient, factor, aux, wts, own, turn, dinv, basis, dirs, halo, packed,
+    square, series, fourth, left_op, right_op, right_two,
     vol_sem, small_sem, halo_send, halo_recv, sum_send, sum_recv,
 ):
     gx, gy = lax.axis_index("gx"), lax.axis_index("gy")
@@ -141,12 +140,6 @@
         turn[:, at] = jnp.broadcast_to(there, (8, width))
     own[...] = own_part
 
-    for e in range(nz):
-        loads[e].wait()
-        start = e % 2 * NP
-        for v in range(NV):
-            mat[e // 2, v, :, start : start + NP] = held_vol[e, :, v * NP : (v + 1) * NP]
-
     sub = iota((8, lanes), 0)
     low = iota((NP, lanes), 1) < NP
     eye = iota((NP, lanes), 1) % NP == iota((NP, lanes), 0)
@@ -157,19 +150,30 @@
             total = jnp.where(sub == v, parts[v], total)
         return total
 
+    dinv[...] = jnp.zeros_like(dinv)
     for p in range(pairs):
         at = slice(p * lanes, (p + 1) * lanes)
-        diagonal = stack(
-            [
-                jnp.sum(
-                    jnp.where(eye, mat[p, v, v * NP : (v + 1) * NP, :], 0.0), axis=0, keepdims=True
+        loads[2 * p].wait()
+        loads[2 * p + 1].wait()
+        for w in range(NV):
+            cut = slice(w * NP, (w + 1) * NP)
+
+            def tile_of(v):
+                rows = slice(v * NP, (v + 1) * NP)
+                return jnp.concatenate(
+                    [held_vol[2 * p, rows, cut], held_vol[2 * p + 1, rows, cut]], axis=1
                 )
-                for v in range(NV)
-            ]
-        )
-        for v in range(NV):
-            diagonal = diagonal + jnp.where(sub == v, own[v * 8 : v * 8 + 8, at], 0.0)
-        dinv[:, at] = jnp.where(sub < NV, 1.0 / jnp.where(sub < NV, diagonal, 1.0), 0.0)
+
+            middle = tile_of(w)
+            diagonal = jnp.sum(jnp.where(eye, middle, 0.0), axis=0, keepdims=True)
+            inverse = 1.0 / (diagonal + own[w * 9 : w * 9 + 1, at])
+            dinv[w : w + 1, at] = inverse
+            for v in range(NV):
+                if v == w:
+                    tile = jnp.where(eye, 0.0, middle)
+                else:
+                    tile = tile_of(v) + jnp.where(eye, own[w * 8 + v : w * 8 + v + 1, at], 0.0)
+                factor[p, w, v * NP : (v + 1) * NP, :] = -tile * inverse
 
     def dense_product(blocks, value, p):
         at = slice(p * lanes, (p + 1) * lanes)
@@ -184,18 +188,8 @@
             parts.append(jnp.sum(placed, axis=0, keepdims=True))
         return stack(parts)
 
-    def series_product(blocks, value):
+    def power_product(blocks, value):
         return jnp.concatenate([dense_product(blocks, value, p) for p in range(pairs)], axis=1)
-
-    def block_product(value):
-        pieces = []
-        for p in range(pairs):
-            at = slice(p * lanes, (p + 1) * lanes)
-            total = dense_product(mat, value, p)
-            for w in range(NV):
-                total = total + own[w * 8 : w * 8 + 8, at] * value[w : w + 1, at]
-            pieces.append(total)
-        return jnp.concatenate(pieces, axis=1)
 
     def face_product(axis, before, after):
         fixed = axis_coords(iota((8, width), 1) % NP, axis)[0]
@@ -213,40 +207,40 @@
             pieces.append(total)
         return jnp.concatenate(pieces, axis=1)
 
-    def put_right(p, v, w, tile):
+    def put_right(p, v, w, tile, target):
         cut = slice(w * lanes, (w + 1) * lanes)
         upper, lower = slice(v * lanes, v * lanes + NP), slice(v * lanes + NP, (v + 1) * lanes)
-        right_op[p, upper, cut] = jnp.where(low, tile, 0.0).astype(jnp.bfloat16)
-        right_op[p, lower, cut] = jnp.where(low, 0.0, tile).astype(jnp.bfloat16)
-
-    def first_powers():
+        target[p, upper, cut] = jnp.where(low, tile, 0.0).astype(jnp.bfloat16)
+        target[p, lower, cut] = jnp.where(low, 0.0, tile).astype(jnp.bfloat16)
+
+    def operands(p):
+        for w in range(NV):
+            for v in range(NV):
+                rows = slice(v * NP, (v + 1) * NP)
+                tile = factor[p, w, rows, :]
+                left_op[p, rows, w * lanes : (w + 1) * lanes] = tile.astype(jnp.bfloat16)
+                put_right(p, v, w, tile, right_op)
+
+    def square_of(p):
+        product = jnp.dot(left_op[p, 0:BLK, :], right_op[p], preferred_element_type=jnp.float32)
+        for w in range(NV):
+            square[p, w] = product[:, w * lanes : (w + 1) * lanes]
+
+    def more_powers():
         for p in range(pairs):
             for w in range(NV):
-                at = slice(p * lanes, (p + 1) * lanes)
                 for v in range(NV):
                     rows = slice(v * NP, (v + 1) * NP)
-                    tile = mat[p, w, rows, :]
-                    if v == w:
-                        tile = jnp.where(eye, 0.0, tile)
-                    else:
-                        tile = tile + jnp.where(eye, own[w * 8 + v : w * 8 + v + 1, at], 0.0)
-                    tile = -tile * dinv[w : w + 1, at]
-                    series[p, w, rows, :] = tile
-                    left_op[p, rows, w * lanes : (w + 1) * lanes] = tile.astype(jnp.bfloat16)
-                    put_right(p, v, w, tile)
-        for p in range(pairs):
-            square = jnp.dot(left_op[p, 0:BLK, :], right_op[p], preferred_element_type=jnp.float32)
+                    tile = square[p, w, rows, :]
+                    left_op[p, BLK + v * NP : BLK + (v + 1) * NP, w * lanes : (w + 1) * lanes] = (
+                        tile.astype(jnp.bfloat16)
+                    )
+                    put_right(p, v, w, tile, right_two)
+        for p in range(pairs):
+            both = jnp.dot(left_op[p], right_two[p], preferred_element_type=jnp.float32)
             for w in range(NV):
                 cut = slice(w * lanes, (w + 1) * lanes)
-                series[p, w] = series[p, w] + square[:, cut]
-                left_op[p, BLK : 2 * BLK, cut] = square[:, cut].astype(jnp.bfloat16)
-                for v in range(NV):
-                    put_right(p, v, w, square[v * NP : (v + 1) * NP, cut])
-        for p in range(pairs):
-            both = jnp.dot(left_op[p], right_op[p], preferred_element_type=jnp.float32)
-            for w in range(NV):
-                cut = slice(w * lanes, (w + 1) * lanes)
-                series[p, w] = series[p, w] + both[0:BLK, cut]
+                series[p, w] = factor[p, w] + square[p, w] + both[0:BLK, cut]
                 fourth[p, w] = both[BLK : 2 * BLK, cut]
 
     def all_powers():
@@ -255,7 +249,7 @@
                 cut = slice(w * lanes, (w + 1) * lanes)
                 left_op[p, 0:BLK, cut] = fourth[p, w].astype(jnp.bfloat16)
                 for v in range(NV):
-                    put_right(p, v, w, series[p, w, v * NP : (v + 1) * NP, :])
+                    put_right(p, v, w, series[p, w, v * NP : (v + 1) * NP, :], right_op)
         for p in range(pairs):
             last = jnp.dot(left_op[p, 0:BLK, :], right_op[p], preferred_element_type=jnp.float32)
             for w in range(NV):
@@ -291,11 +285,12 @@
             device_id_type=MESH,
         )
 
-    def apply_jacobian(step, meanwhile):
+    def apply_jacobian(step, solved, meanwhile):
+        direction = dinv[...] * solved
+        dirs[step] = direction
         for side in range(sides):
             halo_copy(step, side).start()
-        direction = dirs[step]
-        inner_part = block_product(direction) - basis[step]
+        inner_part = (solved - basis[step]) - power_product(factor, solved)
         before, after = pltpu.roll(direction, NP, 1), pltpu.roll(direction, width - NP, 1)
         inner_part = inner_part + face_product(2, before, after)
         meanwhile()
@@ -307,25 +302,26 @@
             + face_product(1, halo[step, 2], halo[step, sides - 1])
         )
 
-    state[...] = dinv[...] * basis[0]
-
-    def sweep(_, inner):
-        value = state[...]
-        state[...] = value + dinv[...] * (basis[0] - block_product(value))
-        return inner
-
-    lax.fori_loop(0, SWEEPS, sweep, 0)
-    dirs[0] = state[...]
+    begun = basis[0]
+    solved = begun
+    for sweep in range(3):
+        solved = begun + power_product(factor, solved)
+        for p in range(pairs):
+            if sweep == p % 2:
+                operands(p)
+            if sweep == p % 2 + 1:
+                square_of(p)
+    solved = solved + power_product(square, power_product(square, solved))
     pl.semaphore_wait(barrier, devices - 1)
-    apply_jacobian(0, first_powers)
-
-    vector = basis[1]
-    vector = vector + series_product(series, vector)
-    dirs[1] = dinv[...] * (vector + series_product(fourth, vector))
-    apply_jacobian(1, all_powers)
-
-    vector = basis[2]
-    dirs[2] = dinv[...] * (vector + series_product(series, vector))
+    apply_jacobian(0, solved, more_powers)
+
+    solved = basis[1]
+    solved = solved + power_product(series, solved)
+    solved = solved + power_product(fourth, solved)
+    apply_jacobian(1, solved, all_powers)
+
+    solved = basis[2]
+    solved = solved + power_product(series, solved)
 
     count = ITERS + 1
     where = iota((1, lanes), 1)
@@ -348,7 +344,7 @@
             for at, entry in enumerate([dot(scaled[i], scaled[j]), peaks[i], peaks[j]]):
                 rows[at] = jnp.where(chosen, entry, rows[at])
 
-    apply_jacobian(ITERS - 1, lambda: [add_products(j) for j in range(ITERS)])
+    apply_jacobian(ITERS - 1, solved, lambda: [add_products(j) for j in range(ITERS)])
     add_products(ITERS)
     row, row_peak, column_peak = rows
     packed[me, :, 0:lanes] = row
@@ -448,11 +444,12 @@
                 pltpu.VMEM((8, width), f32),
                 pltpu.VMEM((ITERS + 1, 8, width), f32),
                 pltpu.VMEM((ITERS, 8, width), f32),
-                pltpu.VMEM((8, width), f32),
                 pltpu.VMEM((ITERS, 4, 8, width), f32),
                 pltpu.VMEM((nx * ny, 1, 6 * NP), f32),
                 pltpu.VMEM((nz // 2, NV, NV * NP, 2 * NP), f32),
                 pltpu.VMEM((nz // 2, NV, NV * NP, 2 * NP), f32),
+                pltpu.VMEM((nz // 2, NV, NV * NP, 2 * NP), f32),
+                pltpu.VMEM((nz // 2, 2 * BLK, 2 * BLK), jnp.bfloat16),
                 pltpu.VMEM((nz // 2, 2 * BLK, 2 * BLK), jnp.bfloat16),
                 pltpu.VMEM((nz // 2, 2 * BLK, 2 * BLK), jnp.bfloat16),
                 dma((nz,)),

time: 28.8 us -> 28.2 us (0.979)
  Pallas kernels: 24.9 us -> 24.3 us
    pallas_call x1, Pallas kernels: 24.9 us -> 24.3 us  [body(): pl.pallas_call(lambda *refs: kernel(nx, ny, nz, *refs), out_shape=(jax.Sh...]
where the time goes in v2:
time: 28.2 us; the launch traced here: 28 us
  Pallas kernels  24.3 us (86%)
  between operations  2.4 us (9%)
  local copies, waits for them, and re-layouts  1.29 us (5%)
    pallas_call x1, Pallas kernels, body(): pl.pallas_call(lambda *refs: kernel(nx, ny, nz, *refs), out_shape=(jax.Sh...  24.3 us
    unnamed x1, local copies, waits for them, and re-layouts  1.29 us

profile of v2, /device:TPU:0, one launch (start us, length us, event | category | flops | bytes accessed | tf_op | source)
XLA Modules:
  0.0 28.0 jit_solution(593203011922495557)
XLA Ops:
  0.6 24.3 %newton_step.1 = (f32[1,1,4,320]{3,2,1,0:T(4,128)}, f32[1,1]{1,0:T(1,128)}) custom-call(f32[1,1,4,320,320]{4,3,2,1,0:T(8,128)} %refs_0_.1, f32[1,1,4,320]{3,2,1,0:T(4,128)} %refs_1_.1, f32[5,5,4,6]{3,2,1,0:T(4,128)} %bitcast.4, f32[1,1,4]{2,1,0:T(1,128)} %refs_3_.1, s32[1,1,4,6]{3,2,1,0:T(4,128)} %refs_4_.1), custom_call_target="tpu_custom_call" | custom-call | tf_op jit(solution)/shard_map/newton_step/pallas_call | solution.py:425
  25.0 1.3 %copy.9 = f32[1,1,4,320]{3,2,1,0:T(4,128)} copy(f32[1,1,4,320]{3,2,1,0:T(4,128)} %get-tuple-element.8) | data formatting | bytes 10240

commit v3 on v2

--- a/solution.py
+++ b/solution.py
@@ -18,6 +18,7 @@
 DOWN = 2.0**-40
 TINY = 1e-36
 UNROLL = 64
+GRANT = 24 * 2**20
 
 
 def iota(shape, dim):
@@ -41,7 +42,8 @@
     out, ratio,
     held_vol, rhs, face, inv_step, orient, factor, aux, wts, own, turn, dinv, basis, dirs, halo, packed,
     square, series, fourth, left_op, right_op, right_two,
-    vol_sem, small_sem, halo_send, halo_recv, sum_send, sum_recv,
+    out_held, ratio_held,
+    vol_sem, small_sem, halo_send, halo_recv, sum_send, sum_recv, out_sem,
 ):
     gx, gy = lax.axis_index("gx"), lax.axis_index("gy")
     devices = nx * ny
@@ -401,15 +403,23 @@
         for j in range(i + 1, ITERS):
             left = left - columns[j][i] * solved[j]
         solved[i] = left / columns[i][i]
-    ratio[...] = jnp.abs(target[ITERS]) / upper[0, 0]
+    ratio_held[...] = jnp.abs(target[ITERS]) / upper[0, 0]
     update = solved[0] * (dirs[0] * (1.0 / DOWN))
     for j in range(1, ITERS):
         update = update + solved[j] * (dirs[j] * (sizes[0] / DOWN / sizes[j]))
     for e in range(nz):
         for v in range(NV):
-            out[0, 0, e : e + 1, v * NP : (v + 1) * NP] = update[
+            out_held[0, 0, e : e + 1, v * NP : (v + 1) * NP] = update[
                 v : v + 1, e * NP : (e + 1) * NP
             ]
+    stores = [
+        pltpu.make_async_copy(out_held, out, out_sem.at[0]),
+        pltpu.make_async_copy(ratio_held, ratio, out_sem.at[1]),
+    ]
+    for store in stores:
+        store.start()
+    for store in stores:
+        store.wait()
 
 
 def solution(mesh):
@@ -428,8 +438,8 @@
                 jax.ShapeDtypeStruct(rhs.shape, f32),
                 jax.ShapeDtypeStruct((1, 1), f32),
             ),
-            in_specs=[pl.BlockSpec(memory_space=pl.ANY)] * 5,
-            out_specs=(vmem, vmem),
+            in_specs=[pl.BlockSpec(memory_space=pltpu.HBM)] * 5,
+            out_specs=(pl.BlockSpec(memory_space=pl.ANY), pl.BlockSpec(memory_space=pl.ANY)),
             scratch_shapes=[
                 pltpu.VMEM((nz, NV * NP, NV * NP), f32),
                 pltpu.VMEM(rhs.shape, f32),
@@ -452,16 +462,26 @@
                 pltpu.VMEM((nz // 2, 2 * BLK, 2 * BLK), jnp.bfloat16),
                 pltpu.VMEM((nz // 2, 2 * BLK, 2 * BLK), jnp.bfloat16),
                 pltpu.VMEM((nz // 2, 2 * BLK, 2 * BLK), jnp.bfloat16),
+                pltpu.VMEM(rhs.shape, f32),
+                pltpu.VMEM((1, 1), f32),
                 dma((nz,)),
                 dma((4,)),
                 dma((ITERS, 4)),
                 dma((ITERS, 4)),
                 dma,
                 dma,
+                dma((2,)),
             ],
-            compiler_params=pltpu.CompilerParams(collective_id=0, has_side_effects=True),
+            compiler_params=pltpu.CompilerParams(
+                collective_id=0, has_side_effects=True, vmem_limit_bytes=GRANT
+            ),
             name="newton_step",
-        )(vol_jac, rhs, face, inv_step, orientation)
+        )(
+            *[
+                pltpu.with_memory_space_constraint(value, pltpu.HBM)
+                for value in (vol_jac, rhs, face, inv_step, orientation)
+            ]
+        )
         return update, ratio[0, 0]
 
     placed = (

time: 28.2 us -> 27.3 us (0.968)
  local copies, waits for them, and re-layouts: 1.29 us -> 0.6 us
    unnamed x1, local copies, waits for them, and re-layouts: 1.29 us -> 0.6 us
where the time goes in v3:
time: 27.3 us; the launch traced here: 27.2 us
  Pallas kernels  24.3 us (89%)
  between operations  2.33 us (9%)
  local copies, waits for them, and re-layouts  0.6 us (2%)
    pallas_call x1, Pallas kernels, body(): pl.pallas_call(lambda *refs: kernel(nx, ny, nz, *refs), out_shape=(jax.Sh...  24.3 us
    unnamed x1, local copies, waits for them, and re-layouts  0.6 us

profile of v3, /device:TPU:0, one launch (start us, length us, event | category | flops | bytes accessed | tf_op | source)
XLA Modules:
  0.0 27.2 jit_solution(3967140206800863625)
XLA Ops:
  0.6 24.3 %newton_step.1 = (f32[1,1,4,320]{3,2,1,0:T(4,128)S(1)}, f32[1,1]{1,0:T(1,128)}) custom-call(f32[1,1,4,320,320]{4,3,2,1,0:T(8,128)} %refs_0_.1, f32[1,1,4,320]{3,2,1,0:T(4,128)} %refs_1_.1, f32[5,5,4,6]{3,2,1,0:T(4,128)} %bitcast.4, f32[1,1,4]{2,1,0:T(1,128)} %refs_3_.1, s32[1,1,4,6]{3,2,1,0:T(4,128)} %refs_4_.1), custom_call_target="tpu_custom_call" | custom-call | tf_op jit(solution)/shard_map/newton_step/pallas_call | solution.py:435
  24.9 0.6 %copy.9 = f32[1,1,4,320]{3,2,1,0:T(4,128)} copy(f32[1,1,4,320]{3,2,1,0:T(4,128)S(1)} %get-tuple-element.8) | data formatting | bytes 10240

commit v4 on v3

--- a/solution.py
+++ b/solution.py
@@ -39,10 +39,10 @@
 def kernel(
     nx, ny, nz,
     vol, rhs_in, face_in, step_in, orient_in,
-    out, ratio,
+    out,
     held_vol, rhs, face, inv_step, orient, factor, aux, wts, own, turn, dinv, basis, dirs, halo, packed,
     square, series, fourth, left_op, right_op, right_two,
-    out_held, ratio_held,
+    out_held,
     vol_sem, small_sem, halo_send, halo_recv, sum_send, sum_recv, out_sem,
 ):
     gx, gy = lax.axis_index("gx"), lax.axis_index("gy")
@@ -403,7 +403,9 @@
         for j in range(i + 1, ITERS):
             left = left - columns[j][i] * solved[j]
         solved[i] = left / columns[i][i]
-    ratio_held[...] = jnp.abs(target[ITERS]) / upper[0, 0]
+    out_held[0, 0, nz : nz + 1, :] = jnp.broadcast_to(
+        jnp.abs(target[ITERS]) / upper[0, 0], (1, BLK)
+    )
     update = solved[0] * (dirs[0] * (1.0 / DOWN))
     for j in range(1, ITERS):
         update = update + solved[j] * (dirs[j] * (sizes[0] / DOWN / sizes[j]))
@@ -414,7 +416,6 @@
             ]
     stores = [
         pltpu.make_async_copy(out_held, out, out_sem.at[0]),
-        pltpu.make_async_copy(ratio_held, ratio, out_sem.at[1]),
     ]
     for store in stores:
         store.start()
@@ -432,14 +433,11 @@
         f32 = jnp.float32
         vmem = pl.BlockSpec(memory_space=pltpu.VMEM)
         dma = pltpu.SemaphoreType.DMA
-        update, ratio = pl.pallas_call(
+        result = pl.pallas_call(
             lambda *refs: kernel(nx, ny, nz, *refs),
-            out_shape=(
-                jax.ShapeDtypeStruct(rhs.shape, f32),
-                jax.ShapeDtypeStruct((1, 1), f32),
-            ),
+            out_shape=jax.ShapeDtypeStruct((1, 1, nz + 1, BLK), f32),
             in_specs=[pl.BlockSpec(memory_space=pltpu.HBM)] * 5,
-            out_specs=(pl.BlockSpec(memory_space=pl.ANY), pl.BlockSpec(memory_space=pl.ANY)),
+            out_specs=pl.BlockSpec(memory_space=pl.ANY),
             scratch_shapes=[
                 pltpu.VMEM((nz, NV * NP, NV * NP), f32),
                 pltpu.VMEM(rhs.shape, f32),
@@ -462,15 +460,14 @@
                 pltpu.VMEM((nz // 2, 2 * BLK, 2 * BLK), jnp.bfloat16),
                 pltpu.VMEM((nz // 2, 2 * BLK, 2 * BLK), jnp.bfloat16),
                 pltpu.VMEM((nz // 2, 2 * BLK, 2 * BLK), jnp.bfloat16),
-                pltpu.VMEM(rhs.shape, f32),
-                pltpu.VMEM((1, 1), f32),
+                pltpu.VMEM((1, 1, nz + 1, BLK), f32),
                 dma((nz,)),
                 dma((4,)),
                 dma((ITERS, 4)),
                 dma((ITERS, 4)),
                 dma,
                 dma,
-                dma((2,)),
+                dma((1,)),
             ],
             compiler_params=pltpu.CompilerParams(
                 collective_id=0, has_side_effects=True, vmem_limit_bytes=GRANT
@@ -482,7 +479,7 @@
                 for value in (vol_jac, rhs, face, inv_step, orientation)
             ]
         )
-        return update, ratio[0, 0]
+        return result[:, :, :nz], result[0, 0, nz, 0]
 
     placed = (
         P("gx", "gy", None, None),

time: 27.3 us -> 25.7 us (0.941)
  between operations: 2.33 us -> 0.64 us
  local copies, waits for them, and re-layouts: 0.6 us -> 1.11 us
  Pallas kernels: 24.3 us -> 23.8 us
    slice x0 -> x2, local copies, waits for them, and re-layouts: none -> 1.11 us  [body(): return (result[:, :, :nz], result[0, 0, nz, 0])]
    unnamed x1 -> x0, local copies, waits for them, and re-layouts: 0.6 us -> none
    pallas_call x1, Pallas kernels: 24.3 us -> 23.8 us  [body(): pl.pallas_call(lambda *refs: kernel(nx, ny, nz, *refs), out_shape=jax.Sha...]
where the time goes in v4:
time: 25.7 us; the launch traced here: 25.5 us
  Pallas kernels  23.8 us (93%)
  local copies, waits for them, and re-layouts  1.11 us (4%)
  between operations  0.64 us (2%)
    pallas_call x1, Pallas kernels, body(): pl.pallas_call(lambda *refs: kernel(nx, ny, nz, *refs), out_shape=jax.Sha...  23.8 us
    slice x2, local copies, waits for them, and re-layouts, body(): return (result[:, :, :nz], result[0, 0, nz, 0])  1.11 us

profile of v4, /device:TPU:0, one launch (start us, length us, event | category | flops | bytes accessed | tf_op | source)
XLA Modules:
  0.0 25.5 jit_solution(6110007388887145815)
XLA Ops:
  0.6 23.8 %newton_step.1 = f32[1,1,5,320]{3,2,1,0:T(8,128)S(1)} custom-call(f32[1,1,4,320,320]{4,3,2,1,0:T(8,128)} %refs_0_.1, f32[1,1,4,320]{3,2,1,0:T(4,128)} %refs_1_.1, f32[5,5,4,6]{3,2,1,0:T(4,128)} %bitcast.4, f32[1,1,4]{2,1,0:T(1,128)} %refs_3_.1, s32[1,1,4,6]{3,2,1,0:T(4,128)} %refs_4_.1), custom_call_target="tpu_custom_call" | custom-call | tf_op jit(solution)/shard_map/newton_step/pallas_call | solution.py:436
  24.4 0.5 %slice.7 = f32[1,1,1,1]{3,2,1,0:T(1,128)} slice(f32[1,1,5,320]{3,2,1,0:T(8,128)S(1)} %newton_step.1), slice={[0:1], [0:1], [4:5], [0:1]} | slice | bytes 8 | tf_op jit(solution)/shard_map/slice | solution.py:482
  24.9 0.6 %slice.6 = f32[1,1,4,320]{3,2,1,0:T(4,128)} slice(f32[1,1,5,320]{3,2,1,0:T(8,128)S(1)} %newton_step.1), slice={[0:1], [0:1], [0:4], [0:320]} | slice | bytes 10240 | tf_op jit(solution)/shard_map/slice | solution.py:482

commit v5 on v4

--- a/solution.py
+++ b/solution.py
@@ -421,6 +421,11 @@
         store.start()
     for store in stores:
         store.wait()
+
+
+def hand_out(nz, both, update, ratio):
+    update[...] = both[:, :, 0:nz, :]
+    ratio[...] = both[0, 0, nz : nz + 1, 0:1]
 
 
 def solution(mesh):
@@ -479,7 +484,18 @@
                 for value in (vol_jac, rhs, face, inv_step, orientation)
             ]
         )
-        return result[:, :, :nz], result[0, 0, nz, 0]
+        update, ratio = pl.pallas_call(
+            lambda both, first, second: hand_out(nz, both, first, second),
+            out_shape=(
+                jax.ShapeDtypeStruct(rhs.shape, f32),
+                jax.ShapeDtypeStruct((1, 1), f32),
+            ),
+            in_specs=[vmem],
+            out_specs=(vmem, vmem),
+            compiler_params=pltpu.CompilerParams(vmem_limit_bytes=2**20),
+            name="hand_out",
+        )(result)
+        return update, ratio[0, 0]
 
     placed = (
         P("gx", "gy", None, None),

time: 25.7 us -> 25.2 us (0.981)
  local copies, waits for them, and re-layouts: 1.11 us -> 0 us
  Pallas kernels: 23.8 us -> 24.4 us
    slice x2 -> x0, local copies, waits for them, and re-layouts: 1.11 us -> none  [body(): return (result[:, :, :nz], result[0, 0, nz, 0])]
    pallas_call x0 -> x1, Pallas kernels: none -> 0.6 us  [body(): pl.pallas_call(lambda both, first, second: hand_out(nz, both, first, seco...]
where the time goes in v5:
time: 25.2 us; the launch traced here: 25 us
  Pallas kernels  24.4 us (97%)
  between operations  0.64 us (3%)
    pallas_call x1, Pallas kernels, body(): pl.pallas_call(lambda *refs: kernel(nx, ny, nz, *refs), out_shape=jax.Sha...  23.8 us
    pallas_call x1, Pallas kernels, body(): pl.pallas_call(lambda both, first, second: hand_out(nz, both, first, seco...  0.6 us

profile of v5, /device:TPU:0, one launch (start us, length us, event | category | flops | bytes accessed | tf_op | source)
XLA Modules:
  0.0 25.0 jit_solution(16658051551451124931)
XLA Ops:
  0.6 23.8 %newton_step.1.both = f32[1,1,5,320]{3,2,1,0:T(8,128)S(1)} custom-call(f32[1,1,4,320,320]{4,3,2,1,0:T(8,128)} %refs_0_.1, f32[1,1,4,320]{3,2,1,0:T(4,128)} %refs_1_.1, f32[5,5,4,6]{3,2,1,0:T(4,128)} %bitcast.4, f32[1,1,4]{2,1,0:T(1,128)} %refs_3_.1, s32[1,1,4,6]{3,2,1,0:T(4,128)} %refs_4_.1), custom_call_target="tpu_custom_call" | custom-call | tf_op jit(solution)/shard_map/newton_step/pallas_call | solution.py:441
  24.4 0.6 %hand_out.1 = (f32[1,1,4,320]{3,2,1,0:T(4,128)}, f32[1,1]{1,0:T(1,128)}) custom-call(f32[1,1,5,320]{3,2,1,0:T(8,128)S(1)} %newton_step.1.both), custom_call_target="tpu_custom_call" | custom-call | tf_op jit(solution)/shard_map/hand_out/pallas_call | solution.py:487

commit v6 on v5

--- a/solution.py
+++ b/solution.py
@@ -315,12 +315,11 @@
                 square_of(p)
     solved = solved + power_product(square, power_product(square, solved))
     pl.semaphore_wait(barrier, devices - 1)
-    apply_jacobian(0, solved, more_powers)
+    apply_jacobian(0, solved, lambda: [more_powers(), all_powers()])
 
     solved = basis[1]
     solved = solved + power_product(series, solved)
-    solved = solved + power_product(fourth, solved)
-    apply_jacobian(1, solved, all_powers)
+    apply_jacobian(1, solved, lambda: None)
 
     solved = basis[2]
     solved = solved + power_product(series, solved)

time: 25.2 us -> 24.9 us (0.988)
  Pallas kernels: 24.4 us -> 24.1 us
    pallas_call x1, Pallas kernels: 23.8 us -> 23.5 us  [body(): pl.pallas_call(lambda *refs: kernel(nx, ny, nz, *refs), out_shape=jax.Sha...]
where the time goes in v6:
time: 24.9 us; the launch traced here: 24.7 us
  Pallas kernels  24.1 us (97%)
  between operations  0.64 us (3%)
    pallas_call x1, Pallas kernels, body(): pl.pallas_call(lambda *refs: kernel(nx, ny, nz, *refs), out_shape=jax.Sha...  23.5 us
    pallas_call x1, Pallas kernels, body(): pl.pallas_call(lambda both, first, second: hand_out(nz, both, first, seco...  0.6 us

profile of v6, /device:TPU:0, one launch (start us, length us, event | category | flops | bytes accessed | tf_op | source)
XLA Modules:
  0.0 24.7 jit_solution(9642908716570340667)
XLA Ops:
  0.6 23.5 %newton_step.1.both = f32[1,1,5,320]{3,2,1,0:T(8,128)S(1)} custom-call(f32[1,1,4,320,320]{4,3,2,1,0:T(8,128)} %refs_0_.1, f32[1,1,4,320]{3,2,1,0:T(4,128)} %refs_1_.1, f32[5,5,4,6]{3,2,1,0:T(4,128)} %bitcast.4, f32[1,1,4]{2,1,0:T(1,128)} %refs_3_.1, s32[1,1,4,6]{3,2,1,0:T(4,128)} %refs_4_.1), custom_call_target="tpu_custom_call" | custom-call | tf_op jit(solution)/shard_map/newton_step/pallas_call | solution.py:440
  24.1 0.6 %hand_out.1 = (f32[1,1,4,320]{3,2,1,0:T(4,128)}, f32[1,1]{1,0:T(1,128)}) custom-call(f32[1,1,5,320]{3,2,1,0:T(8,128)S(1)} %newton_step.1.both), custom_call_target="tpu_custom_call" | custom-call | tf_op jit(solution)/shard_map/hand_out/pallas_call | solution.py:486
